TPU v7x, 256 devices: a whole 4x4x8 slice. The times are simulated.
256 devices in a mesh: row: 32 (over y, z), col: 8 (over x, core).
Axes of the slice: x: 4, y: 4, z: 8, core: 2. Of those that a mesh axis runs over, the one named last changes fastest.
Arguments:
- embedding: bfloat16 [8, 32, 48, 256], P('col', 'row'), may hold values from -0.3984375 to 0.3984375
- preference: float32 [12288], P('row'), may hold values from -2.5 to -0.5
Outputs:
- responsibility: float32 [12288, 12288], P('row', 'col')
- availability: float32 [12288, 12288], P('row', 'col')
All inputs are finite; a program needn't handle non-finite values.
Results may differ from a plain program's by a relative error of at most 0.0003.
Values may be sent and summed in bfloat16 or wider, within the bound.
A program may use at most 64 MiB of HBM per device.

v0:
```python
import jax
import jax.numpy as jnp
from jax import lax
from jax.sharding import PartitionSpec as P

ITERS = 2
DAMPING = 0.5


def broadcast(block, axis, source):
    block = jnp.where(lax.axis_index(axis) == source, block, jnp.zeros_like(block))
    return lax.psum(block, axis)


def similarity(row_emb, col_emb, row_start, col_start, pref_rows):
    cross = lax.dot_general(
        row_emb, col_emb, (((1,), (1,)), ((), ())), preferred_element_type=jnp.float32
    )
    row_vals = row_emb.astype(jnp.float32)
    col_vals = col_emb.astype(jnp.float32)
    row_sq = jnp.sum(row_vals * row_vals, axis=1)
    col_sq = jnp.sum(col_vals * col_vals, axis=1)
    dist = 2.0 * cross - row_sq[:, None] - col_sq[None, :]
    row_ids = row_start + jnp.arange(row_emb.shape[0], dtype=jnp.int32)
    col_ids = col_start + jnp.arange(col_emb.shape[0], dtype=jnp.int32)
    diagonal = row_ids[:, None] == col_ids[None, :]
    return (jnp.where(diagonal, pref_rows[:, None], dist), diagonal)


def top_two(summed):
    first = jnp.max(summed, axis=1)
    hits = summed == first[:, None]
    repeats = jnp.sum(hits.astype(jnp.int32), axis=1)
    others = jnp.max(jnp.where(hits, -jnp.inf, summed), axis=1)
    second = jnp.where(repeats > 1, first, others)
    return (first, second)


def local(embedding, preference):
    rows_n = lax.axis_size("row")
    cols_n = lax.axis_size("col")
    row_idx = lax.axis_index("row")
    col_idx = lax.axis_index("col")
    mol = embedding.shape[2]
    width = embedding.shape[3]
    row_count = mol * cols_n
    col_count = mol * rows_n
    column_block = lax.all_gather(embedding, "row", axis=1, tiled=True).reshape(col_count, width)
    offset = row_idx * cols_n % rows_n
    root = row_idx * cols_n // rows_n
    own_slice = lax.dynamic_slice_in_dim(column_block, offset * mol, row_count, 0)
    row_block = broadcast(own_slice, "col", root)
    row_start = row_idx * row_count
    col_start = col_idx * col_count
    sim, diagonal = similarity(row_block, column_block, row_start, col_start, preference)
    resp = jnp.zeros_like(sim)
    avail = jnp.zeros_like(sim)
    for step in range(ITERS):
        summed = avail + sim
        local_first, local_second = top_two(summed)
        firsts, seconds = (
            lax.all_gather(local_first, "col", axis=0, tiled=True),
            lax.all_gather(local_second, "col", axis=0, tiled=True),
        )
        firsts = firsts.reshape(cols_n, row_count)
        seconds = seconds.reshape(cols_n, row_count)
        first = jnp.max(firsts, axis=0)
        at_top = firsts == first[None, :]
        repeats = jnp.sum(at_top.astype(jnp.int32), axis=0)
        others = jnp.max(jnp.where(at_top, -jnp.inf, firsts), axis=0)
        second = jnp.where(repeats > 1, first, jnp.maximum(jnp.max(seconds, axis=0), others))
        fresh = sim - jnp.where(summed == first[:, None], second[:, None], first[:, None])
        resp = DAMPING * resp + (1.0 - DAMPING) * fresh
        positive = jnp.where(diagonal, resp, jnp.maximum(resp, 0.0))
        colsum = lax.psum(jnp.sum(positive, axis=0), "row")
        renew = colsum[None, :] - positive
        renew = jnp.where(diagonal, renew, jnp.minimum(renew, 0.0))
        avail = DAMPING * avail + (1.0 - DAMPING) * renew
    return (resp, avail)


def solution(mesh):
    placed = (P("col", "row", None, None), P("row"))
    return jax.shard_map(
        local,
        mesh=mesh,
        in_specs=placed,
        out_specs=(P("row", "col"), P("row", "col")),
        check_vma=False,
    )
```

profile of v0, /device:TPU:32, one launch (start us, length us, event | category | flops | bytes accessed | tf_op | source)
XLA Modules:
  0.0 337.2 jit_solution(9302854536227118023)
XLA Ops:
  7.2 0.0 copy-start.1
  7.2 0.0 all-reduce.2.cloned.1.call-start
  7.2 52.2 %all_gather.15 = bf16[1,32,48,256]{3,2,0,1:T(8,128)(2,1)S(1)} all-gather(bf16[1,1,48,256]{3,2,0,1:T(8,128)(2,1)} %bitcast.12), channel_id=1, replica_groups=mesh['row'=32,'col'=8] {'row'}, dimensions={1}, use_global_device_ids=true | all-gather | bytes 811008 | tf_op jit(solution)/shard_map/all_gather | solution.py:48
  59.5 0.7 dynamic-slice_select_fusion
  60.2 0.0 all-reduce.2.cloned.1.call-update
  60.2 0.3 multiply_reduce_fusion
  60.5 0.1 sub.47
  60.6 62.6 %all-reduce.2.cloned.1.call-done = bf16[384,256]{1,0:T(8,128)(2,1)} async-done(((bf16[384,256]{1,0:T(8,128)(2,1)}), bf16[384,256]{1,0:T(8,128)(2,1)}) %all-reduce.2.cloned.1.call-update) | async-done | bytes 196624 | tf_op jit(solution)/shard_map/psum | solution.py:12
  123.2 1.1 multiply_reduce_fusion.1
  124.2 0.0 copy-done.1
  124.3 1.7 fusion.15
  126.0 0.4 fusion.3
  126.4 0.4 fusion.2
  126.8 11.2 %all-gather = f32[8,1,384]{2,1,0:T(1,128)S(1)} all-gather(f32[1,1,384]{2,1,0:T(1,128)S(1)} %reshape.67), channel_id=1, replica_groups=mesh['row'=32,'col'=8] {'col'}, dimensions={0}, use_global_device_ids=true | all-gather | bytes 13824 | tf_op jit(solution)/shard_map/all_gather | solution.py:62
  138.1 11.2 %all-gather.1 = f32[8,1,384]{2,1,0:T(1,128)S(1)} all-gather(f32[1,1,384]{2,1,0:T(1,128)S(1)} %reshape.69), channel_id=1, replica_groups=mesh['row'=32,'col'=8] {'col'}, dimensions={0}, use_global_device_ids=true | all-gather | bytes 13824 | tf_op jit(solution)/shard_map/all_gather | solution.py:63
  149.3 0.7 fusion.9
  150.1 72.6 %psum.22 = f32[1536]{0:T(1024)S(1)} all-reduce(f32[1536]{0:T(1024)S(1)} %fusion.9), channel_id=1, replica_groups=mesh['row'=32,'col'=8] {'row'}, use_global_device_ids=true, to_apply=%region_11.12 | all-reduce | flops 1536 | bytes 12288 | tf_op jit(solution)/shard_map/psum | solution.py:75
  222.7 1.3 fusion.14
  224.0 0.0 copy-start
  224.0 0.4 fusion.4
  224.4 0.4 fusion.5
  224.8 0.6 copy-done
  225.4 11.2 %all-gather.2 = f32[8,1,384]{2,1,0:T(1,128)S(1)} all-gather(f32[1,1,384]{2,1,0:T(1,128)S(1)} %reshape.71), channel_id=1, replica_groups=mesh['row'=32,'col'=8] {'col'}, dimensions={0}, use_global_device_ids=true | all-gather | bytes 13824 | tf_op jit(solution)/shard_map/all_gather | solution.py:62
  236.7 11.2 %all-gather.3 = f32[8,1,384]{2,1,0:T(1,128)S(1)} all-gather(f32[1,1,384]{2,1,0:T(1,128)S(1)} %reshape.73), channel_id=1, replica_groups=mesh['row'=32,'col'=8] {'col'}, dimensions={0}, use_global_device_ids=true | all-gather | bytes 13824 | tf_op jit(solution)/shard_map/all_gather | solution.py:63
  247.9 3.5 %fusion.8 = (f32[1536]{0:T(1024)S(1)}, f32[384,1536]{1,0:T(8,128)}) fusion(s32[1536]{0:T(1024)S(1)} %iota_add_fusion, s32[384]{0:T(512)S(1)} %iota_add_fusion.1, f32[384,1536]{1,0:T(8,128)S(1)} %get-tuple-element.7, f32[384]{0:T(512)S(1)} %maximum_select_fusion, f32[384,1536]{1,0:T(8,128)} %copy-done, f32[384]{0:T(512)S(1)} %reduce_max.96, ...), kind=kLoop, calls=%fused_computation.21 | loop fusion | flops 7666176 | bytes 7097856 | tf_op jit(solution)/shard_map/reduce_sum | solution.py:75
  251.4 74.6 %psum.23 = f32[1536]{0:T(1024)S(1)} all-reduce(f32[1536]{0:T(1024)S(1)} %get-tuple-element.2), channel_id=1, replica_groups=mesh['row'=32,'col'=8] {'row'}, use_global_device_ids=true, to_apply=%region_20.21 | all-reduce | flops 1536 | bytes 12288 | tf_op jit(solution)/shard_map/psum | solution.py:75
  326.0 4.3 %fusion.7 = f32[384,1536]{1,0:T(8,128)} fusion(f32[384,1536]{1,0:T(8,128)} %get-tuple-element.3, f32[384,1536]{1,0:T(8,128)S(1)} %get-tuple-element.7, f32[1536]{0:T(1024)S(1)} %psum.23, f32[1536]{0:T(1024)S(1)} %psum.22, f32[384]{0:T(512)S(1)} %maximum_select_fusion.1, f32[384]{0:T(512)S(1)} %reduce_max.91, s32[1536]{0:T(1024)S(1)} %iota_add_fusion, ...), kind=kLoop, calls=%fused_computation.17 | loop fusion | flops 10616832 | bytes 7100928 | tf_op jit(solution)/shard_map/add | solution.py:78
  (18 shorter events, 0.2 us)
Async XLA Ops:
  7.2 117.1 %copy-start.1 = (f32[384]{0:T(512)S(1)}, f32[384]{0:T(512)}, u32[]{:S(2)}) copy-start(f32[384]{0:T(512)} %param.3) | copy-start | bytes 4612
  7.2 116.0 %all-reduce.2.cloned.1.call-start = ((), (), s32[]{:S(2)}) async-start(), calls=%async_computation | async-start | bytes 393216 | tf_op jit(solution)/shard_map/psum | solution.py:12
  224.0 1.4 copy-start
Sparse Core Ops, SparseCore 0:
  60.3 62.7 all-reduce.1
where the time goes:
time: 338 us; the launch traced here: 337 us
  blocking collectives  244 us (72%)
  waiting for transfers between devices  62.6 us (19%)
  between operations  14.2 us (4%)
  other arithmetic  13.7 us (4%)
    psum x2, blocking collectives, local(): colsum = lax.psum(jnp.sum(positive, axis=0), 'row')  147 us
    psum x1, waiting for transfers between devices, broadcast(): return lax.psum(block, axis)  62.6 us
    all_gather x1, blocking collectives, local(): lax.all_gather(embedding, 'row', axis=1, tiled=True)  52.2 us
    all_gather x2, blocking collectives, local(): lax.all_gather(local_second, 'col', axis=0, tiled=True)  22.4 us
    all_gather x2, blocking collectives, local(): lax.all_gather(local_first, 'col', axis=0, tiled=True)  22.4 us
  transfers between devices with their start and end apart: 1, of which 1 were waited for; matrix products, arithmetic and copies ran while one was open for 0% of the time, Pallas kernels for 0%

commit v1 on v0

--- a/solution.py
+++ b/solution.py
@@ -72,7 +72,7 @@
         fresh = sim - jnp.where(summed == first[:, None], second[:, None], first[:, None])
         resp = DAMPING * resp + (1.0 - DAMPING) * fresh
         positive = jnp.where(diagonal, resp, jnp.maximum(resp, 0.0))
-        colsum = lax.psum(jnp.sum(positive, axis=0), "row")
+        colsum = jnp.sum(lax.all_gather(jnp.sum(positive, axis=0), "row"), axis=0)
         renew = colsum[None, :] - positive
         renew = jnp.where(diagonal, renew, jnp.minimum(renew, 0.0))
         avail = DAMPING * avail + (1.0 - DAMPING) * renew

time: 338 us -> 284 us (0.84)
  blocking collectives: 244 us -> 190 us
    psum x2 -> x0, blocking collectives: 147 us -> none  [local(): colsum = lax.psum(jnp.sum(positive, axis=0), 'row')]
    all_gather x0 -> x2, blocking collectives: none -> 93.4 us  [local(): colsum = jnp.sum(lax.all_gather(jnp.sum(positive, axis=0), 'row'), axis=0)]
where the time goes in v1:
time: 284 us
  blocking collectives  190 us (67%)
  waiting for transfers between devices  62.6 us (22%)
  between operations  14.2 us (5%)
  other arithmetic  14 us (5%)
    all_gather x2, blocking collectives, local(): colsum = jnp.sum(lax.all_gather(jnp.sum(positive, axis=0), 'row'), axis=0)  93.4 us
    psum x1, waiting for transfers between devices, broadcast(): return lax.psum(block, axis)  62.6 us
    all_gather x1, blocking collectives, local(): lax.all_gather(embedding, 'row', axis=1, tiled=True)  52.2 us
    all_gather x2, blocking collectives, local(): lax.all_gather(local_second, 'col', axis=0, tiled=True)  22.4 us
    all_gather x2, blocking collectives, local(): lax.all_gather(local_first, 'col', axis=0, tiled=True)  22.4 us
  transfers between devices with their start and end apart: 1, of which 1 were waited for; matrix products, arithmetic and copies ran while one was open for 0% of the time, Pallas kernels for 0%

profile of v1, /device:TPU:32, one launch (start us, length us, event | category | flops | bytes accessed | tf_op | source)
XLA Modules:
  0.0 283.6 jit_solution(13357901692534469251)
XLA Ops:
  7.2 0.0 copy-start.1
  7.2 0.0 all-reduce.2.cloned.1.call-start
  7.2 52.2 %all_gather.27 = bf16[1,32,48,256]{3,2,0,1:T(8,128)(2,1)S(1)} all-gather(bf16[1,1,48,256]{3,2,0,1:T(8,128)(2,1)} %bitcast.12), channel_id=1, replica_groups=mesh['row'=32,'col'=8] {'row'}, dimensions={1}, use_global_device_ids=true | all-gather | bytes 811008 | tf_op jit(solution)/shard_map/all_gather | solution.py:48
  59.5 0.7 dynamic-slice_select_fusion
  60.2 0.0 all-reduce.2.cloned.1.call-update
  60.2 0.3 multiply_reduce_fusion
  60.5 0.1 sub.47
  60.6 62.6 %all-reduce.2.cloned.1.call-done = bf16[384,256]{1,0:T(8,128)(2,1)} async-done(((bf16[384,256]{1,0:T(8,128)(2,1)}), bf16[384,256]{1,0:T(8,128)(2,1)}) %all-reduce.2.cloned.1.call-update) | async-done | bytes 196624 | tf_op jit(solution)/shard_map/psum | solution.py:12
  123.2 1.1 multiply_reduce_fusion.1
  124.2 0.0 copy-done.1
  124.3 1.7 fusion.15
  126.0 0.4 fusion.3
  126.4 0.4 fusion.2
  126.8 11.2 %all-gather.2 = f32[8,1,384]{2,1,0:T(1,128)S(1)} all-gather(f32[1,1,384]{2,1,0:T(1,128)S(1)} %reshape.69), channel_id=1, replica_groups=mesh['row'=32,'col'=8] {'col'}, dimensions={0}, use_global_device_ids=true | all-gather | bytes 13824 | tf_op jit(solution)/shard_map/all_gather | solution.py:62
  138.1 11.2 %all-gather.3 = f32[8,1,384]{2,1,0:T(1,128)S(1)} all-gather(f32[1,1,384]{2,1,0:T(1,128)S(1)} %reshape.71), channel_id=1, replica_groups=mesh['row'=32,'col'=8] {'col'}, dimensions={0}, use_global_device_ids=true | all-gather | bytes 13824 | tf_op jit(solution)/shard_map/all_gather | solution.py:63
  149.3 0.7 fusion.9
  150.1 47.6 %all-gather.4 = f32[32,1,1536]{2,1,0:T(1,128)S(1)} all-gather(f32[1,1,1536]{2,1,0:T(1,128)S(1)} %reshape.73), channel_id=2, replica_groups=mesh['row'=32,'col'=8] {'row'}, dimensions={0}, use_global_device_ids=true | all-gather | bytes 202752 | tf_op jit(solution)/shard_map/all_gather | solution.py:75
  197.7 0.1 reduce_sum.95
  197.8 1.3 fusion.14
  199.1 0.0 copy-start
  199.1 0.4 fusion.4
  199.5 0.4 fusion.5
  199.9 0.6 copy-done
  200.5 11.2 %all-gather.5 = f32[8,1,384]{2,1,0:T(1,128)S(1)} all-gather(f32[1,1,384]{2,1,0:T(1,128)S(1)} %reshape.75), channel_id=1, replica_groups=mesh['row'=32,'col'=8] {'col'}, dimensions={0}, use_global_device_ids=true | all-gather | bytes 13824 | tf_op jit(solution)/shard_map/all_gather | solution.py:62
  211.8 11.2 %all-gather.6 = f32[8,1,384]{2,1,0:T(1,128)S(1)} all-gather(f32[1,1,384]{2,1,0:T(1,128)S(1)} %reshape.77), channel_id=1, replica_groups=mesh['row'=32,'col'=8] {'col'}, dimensions={0}, use_global_device_ids=true | all-gather | bytes 13824 | tf_op jit(solution)/shard_map/all_gather | solution.py:63
  223.0 3.5 %fusion.8 = (f32[1536]{0:T(1024)S(1)}, f32[384,1536]{1,0:T(8,128)}) fusion(s32[1536]{0:T(1024)S(1)} %iota_add_fusion, s32[384]{0:T(512)S(1)} %iota_add_fusion.1, f32[384,1536]{1,0:T(8,128)S(1)} %get-tuple-element.7, f32[384]{0:T(512)S(1)} %maximum_select_fusion, f32[384,1536]{1,0:T(8,128)} %copy-done, f32[384]{0:T(512)S(1)} %reduce_max.96, ...), kind=kLoop, calls=%fused_computation.21 | loop fusion | flops 7666176 | bytes 7097856 | tf_op jit(solution)/shard_map/reduce_sum | solution.py:75
  226.5 45.8 %all-gather.7 = f32[32,1,1536]{2,1,0:T(1,128)S(1)} all-gather(f32[1,1,1536]{2,1,0:T(1,128)S(1)} %reshape.79), channel_id=3, replica_groups=mesh['row'=32,'col'=8] {'row'}, dimensions={0}, use_global_device_ids=true | all-gather | bytes 202752 | tf_op jit(solution)/shard_map/all_gather | solution.py:75
  272.3 0.1 reduce_sum.99
  272.4 4.3 %fusion.7 = f32[384,1536]{1,0:T(8,128)} fusion(f32[384,1536]{1,0:T(8,128)} %get-tuple-element.3, f32[384,1536]{1,0:T(8,128)S(1)} %get-tuple-element.7, f32[1536]{0:T(1024)S(1)} %reduce_sum.99, f32[1536]{0:T(1024)S(1)} %reduce_sum.95, f32[384]{0:T(512)S(1)} %maximum_select_fusion.1, f32[384]{0:T(512)S(1)} %reduce_max.91, s32[1536]{0:T(1024)S(1)} %iota_add_fusion, ...), kind=kLoop, calls=%fused_computation.17 | loop fusion | flops 10616832 | bytes 7100928 | tf_op jit(solution)/shard_map/add | solution.py:78
  (20 shorter events, 0.3 us)
Async XLA Ops:
  7.2 117.1 %copy-start.1 = (f32[384]{0:T(512)S(1)}, f32[384]{0:T(512)}, u32[]{:S(2)}) copy-start(f32[384]{0:T(512)} %param.3) | copy-start | bytes 4612
  7.2 116.0 %all-reduce.2.cloned.1.call-start = ((), (), s32[]{:S(2)}) async-start(), calls=%async_computation | async-start | bytes 393216 | tf_op jit(solution)/shard_map/psum | solution.py:12
  199.1 1.4 copy-start
Sparse Core Ops, SparseCore 0:
  60.3 62.7 all-reduce.1

commit v2 on v0

--- a/solution.py
+++ b/solution.py
@@ -59,7 +59,9 @@
         summed = avail + sim
         local_first, local_second = top_two(summed)
         firsts, seconds = (
-            lax.all_gather(local_first, "col", axis=0, tiled=True),
+            jnp.concatenate(
+                lax.all_to_all(jnp.stack([local_first] * lax.axis_size("col")), "col", 0, 0), axis=0
+            ),
             lax.all_gather(local_second, "col", axis=0, tiled=True),
         )
         firsts = firsts.reshape(cols_n, row_count)

time: 338 us -> 325 us (0.962)
  blocking collectives: 244 us -> 224 us
  starting transfers between devices: 0.04 us -> 6.71 us
    all_gather x2 -> x0, blocking collectives: 22.4 us -> none  [local(): lax.all_gather(local_first, 'col', axis=0, tiled=True)]
    all_to_all x0 -> x2, starting transfers between devices: none -> 6.68 us  [local(): lax.all_to_all(jnp.stack([local_first] * lax.axis_size('col')), 'col', 0, 0)]
  transfers between devices with their start and end apart: 1 -> 3, of which waited for: 1 -> 1; matrix products, arithmetic and copies ran while one was open for 0% -> 0% of each run, Pallas kernels for 0% -> 0%
where the time goes in v2:
time: 325 us
  blocking collectives  224 us (69%)
  waiting for transfers between devices  62.6 us (19%)
  between operations  14.2 us (4%)
  other arithmetic  13.7 us (4%)
  starting transfers between devices  6.71 us (2%)
    psum x2, blocking collectives, local(): colsum = lax.psum(jnp.sum(positive, axis=0), 'row')  147 us
    psum x1, waiting for transfers between devices, broadcast(): return lax.psum(block, axis)  62.6 us
    all_gather x1, blocking collectives, local(): lax.all_gather(embedding, 'row', axis=1, tiled=True)  52.2 us
    all_gather x2, blocking collectives, local(): lax.all_gather(local_second, 'col', axis=0, tiled=True)  24.5 us
    all_to_all x2, starting transfers between devices, local(): lax.all_to_all(jnp.stack([local_first] * lax.axis_size('col')), 'col', 0, 0)  6.68 us
  transfers between devices with their start and end apart: 3, of which 1 were waited for; matrix products, arithmetic and copies ran while one was open for 0% of the time, Pallas kernels for 0%

profile of v2, /device:TPU:32, one launch (start us, length us, event | category | flops | bytes accessed | tf_op | source)
XLA Modules:
  0.0 324.8 jit_solution(3926164239263136791)
XLA Ops:
  7.2 0.0 copy-start.1
  7.2 0.0 all-reduce.2.cloned.1.call-start
  7.2 52.2 %all_gather.9 = bf16[1,32,48,256]{3,2,0,1:T(8,128)(2,1)S(1)} all-gather(bf16[1,1,48,256]{3,2,0,1:T(8,128)(2,1)} %bitcast.12), channel_id=1, replica_groups=mesh['row'=32,'col'=8] {'row'}, dimensions={1}, use_global_device_ids=true | all-gather | bytes 811008 | tf_op jit(solution)/shard_map/all_gather | solution.py:48
  59.5 0.7 dynamic-slice_select_fusion
  60.2 0.0 all-reduce.2.cloned.1.call-update
  60.2 0.3 multiply_reduce_fusion
  60.5 0.1 sub.47
  60.6 62.6 %all-reduce.2.cloned.1.call-done = bf16[384,256]{1,0:T(8,128)(2,1)} async-done(((bf16[384,256]{1,0:T(8,128)(2,1)}), bf16[384,256]{1,0:T(8,128)(2,1)}) %all-reduce.2.cloned.1.call-update) | async-done | bytes 196624 | tf_op jit(solution)/shard_map/psum | solution.py:12
  123.2 1.1 multiply_reduce_fusion.1
  124.2 0.0 copy-done.1
  124.2 1.7 fusion.15
  126.0 0.4 fusion.3
  126.4 0.4 fusion.2
  126.8 0.6 stack.4
  127.4 3.3 %all-to-all-start = ((f32[8,1,384]{2,1,0:T(1,128)}), f32[8,1,384]{2,1,0:T(1,128)S(1)}, u32[]{:S(2)}, u32[]{:S(2)}) async-start(f32[8,1,384]{2,1,0:T(1,128)} %stack.4), calls=%async_computation | async-start | bytes 24576 | tf_op jit(solution)/shard_map/all_to_all | solution.py:63
  130.8 12.2 %all-gather = f32[8,1,384]{2,1,0:T(1,128)S(1)} all-gather(f32[1,1,384]{2,1,0:T(1,128)S(1)} %reshape.73), channel_id=1, replica_groups=mesh['row'=32,'col'=8] {'col'}, dimensions={0}, use_global_device_ids=true | all-gather | bytes 13824 | tf_op jit(solution)/shard_map/all_gather | solution.py:65
  143.0 0.0 all-to-all-done
  143.1 0.7 fusion.9
  143.9 72.6 %psum.22 = f32[1536]{0:T(1024)S(1)} all-reduce(f32[1536]{0:T(1024)S(1)} %fusion.9), channel_id=1, replica_groups=mesh['row'=32,'col'=8] {'row'}, use_global_device_ids=true, to_apply=%region_11.12 | all-reduce | flops 1536 | bytes 12288 | tf_op jit(solution)/shard_map/psum | solution.py:77
  216.5 1.3 fusion.14
  217.7 0.0 copy-start
  217.8 0.4 fusion.4
  218.2 0.4 fusion.5
  218.6 0.6 copy-done
  219.2 0.6 stack.5
  219.8 3.3 %all-to-all-start.1 = ((f32[8,1,384]{2,1,0:T(1,128)}), f32[8,1,384]{2,1,0:T(1,128)S(1)}, u32[]{:S(2)}, u32[]{:S(2)}) async-start(f32[8,1,384]{2,1,0:T(1,128)} %stack.5), calls=%async_computation.1 | async-start | bytes 24576 | tf_op jit(solution)/shard_map/all_to_all | solution.py:63
  223.1 12.3 %all-gather.1 = f32[8,1,384]{2,1,0:T(1,128)S(1)} all-gather(f32[1,1,384]{2,1,0:T(1,128)S(1)} %reshape.75), channel_id=1, replica_groups=mesh['row'=32,'col'=8] {'col'}, dimensions={0}, use_global_device_ids=true | all-gather | bytes 13824 | tf_op jit(solution)/shard_map/all_gather | solution.py:65
  235.5 0.0 all-to-all-done.1
  235.6 3.5 %fusion.8 = (f32[1536]{0:T(1024)S(1)}, f32[384,1536]{1,0:T(8,128)}) fusion(s32[1536]{0:T(1024)S(1)} %iota_add_fusion, s32[384]{0:T(512)S(1)} %iota_add_fusion.1, f32[384,1536]{1,0:T(8,128)S(1)} %get-tuple-element.7, f32[384]{0:T(512)S(1)} %maximum_select_fusion, f32[384,1536]{1,0:T(8,128)} %copy-done, f32[384]{0:T(512)S(1)} %reduce_max.96, ...), kind=kLoop, calls=%fused_computation.21 | loop fusion | flops 7666176 | bytes 7097856 | tf_op jit(solution)/shard_map/reduce_sum | solution.py:77
  239.1 74.6 %psum.23 = f32[1536]{0:T(1024)S(1)} all-reduce(f32[1536]{0:T(1024)S(1)} %get-tuple-element.2), channel_id=1, replica_groups=mesh['row'=32,'col'=8] {'row'}, use_global_device_ids=true, to_apply=%region_20.21 | all-reduce | flops 1536 | bytes 12288 | tf_op jit(solution)/shard_map/psum | solution.py:77
  313.7 4.3 %fusion.7 = f32[384,1536]{1,0:T(8,128)} fusion(f32[384,1536]{1,0:T(8,128)} %get-tuple-element.3, f32[384,1536]{1,0:T(8,128)S(1)} %get-tuple-element.7, f32[1536]{0:T(1024)S(1)} %psum.23, f32[1536]{0:T(1024)S(1)} %psum.22, f32[384]{0:T(512)S(1)} %maximum_select_fusion.1, f32[384]{0:T(512)S(1)} %reduce_max.91, s32[1536]{0:T(1024)S(1)} %iota_add_fusion, ...), kind=kLoop, calls=%fused_computation.17 | loop fusion | flops 10616832 | bytes 7100928 | tf_op jit(solution)/shard_map/add | solution.py:80
  (16 shorter events, 0.2 us)
Async XLA Ops:
  7.2 117.1 %copy-start.1 = (f32[384]{0:T(512)S(1)}, f32[384]{0:T(512)}, u32[]{:S(2)}) copy-start(f32[384]{0:T(512)} %param.3) | copy-start | bytes 4612
  7.2 116.0 %all-reduce.2.cloned.1.call-start = ((), (), s32[]{:S(2)}) async-start(), calls=%async_computation.2 | async-start | bytes 393216 | tf_op jit(solution)/shard_map/psum | solution.py:12
  127.4 15.6 %all-to-all-start = ((f32[8,1,384]{2,1,0:T(1,128)}), f32[8,1,384]{2,1,0:T(1,128)S(1)}, u32[]{:S(2)}, u32[]{:S(2)}) async-start(f32[8,1,384]{2,1,0:T(1,128)} %stack.4), calls=%async_computation | async-start | bytes 24576 | tf_op jit(solution)/shard_map/all_to_all | solution.py:63
  217.7 1.4 copy-start
  219.8 15.7 %all-to-all-start.1 = ((f32[8,1,384]{2,1,0:T(1,128)}), f32[8,1,384]{2,1,0:T(1,128)S(1)}, u32[]{:S(2)}, u32[]{:S(2)}) async-start(f32[8,1,384]{2,1,0:T(1,128)} %stack.5), calls=%async_computation.1 | async-start | bytes 24576 | tf_op jit(solution)/shard_map/all_to_all | solution.py:63
Sparse Core Ops, SparseCore 0:
  60.3 62.7 all-reduce.1
